TPU v7x, 512 devices: a whole 4x4x16 slice. The times are simulated.
512 devices in a mesh: gx: 128 (over y_hi, z, x), trait: 4 (over y_lo, core).
Axes of the slice: x: 4, y: 4 (y_hi: 2, y_lo: 2; y = y_hi * 2 + y_lo), z: 16, core: 2. Of those that a mesh axis runs over, the one named last changes fastest.
Arguments:
- initial: float32 [1024, 128, 1024], P('gx', None, 'trait'), may hold values from 0.2 to 2
- section_one: float32 [1024, 128, 1024], P('gx', None, 'trait'), may hold values from 0.2 to 2
- section_two: float32 [1024, 128, 1024], P('gx', None, 'trait'), may hold values from 0.2 to 2
- kernels: bfloat16 [2, 1024, 1024], P(None, None, 'trait'), may hold values from -0.1875 to 0.1875
- growth: float32 [1024], P('trait'), may hold values from -3 to 3
- death_rate: float32 [1024], P('trait'), may hold values from 0.5 to 8
Outputs:
- new_one: float32 [1024, 128, 1024], P('gx', None, 'trait')
- new_two: float32 [1024, 128, 1024], P('gx', None, 'trait')
All inputs are finite; a program needn't handle non-finite values.
Results may differ from a plain program's by a relative error of at most 0.002.
Values may be sent and summed in bfloat16 or wider, within the bound.
A program may use at most 64 MiB of HBM per device.

v0:
```python
import jax
import jax.numpy as jnp
from jax import lax
from jax.sharding import PartitionSpec as P

DIFFUSION = 0.25
STEP_SIZE = 0.5


def with_halo(cells, sides, width):
    for axis, dim in sides:
        count = lax.axis_size(axis)
        head = lax.slice_in_dim(cells, 0, width, axis=dim)
        tail = lax.slice_in_dim(cells, cells.shape[dim] - width, cells.shape[dim], axis=dim)
        cells = jnp.concatenate(
            [
                lax.ppermute(tail, axis, [(i, (i + 1) % count) for i in range(count)]),
                cells,
                lax.ppermute(head, axis, [((i + 1) % count, i) for i in range(count)]),
            ],
            axis=dim,
        )
    return cells


def local(initial, section_one, section_two, kernels, growth, death_rate):
    first_dt = STEP_SIZE / 3.0
    second_dt = 2.0 * STEP_SIZE / 3.0

    def products(core):
        xcount, ycount, owned = core.shape
        flat = core.astype(jnp.bfloat16).reshape(xcount * ycount, owned)
        piece = lax.all_gather(flat, "trait", axis=1, tiled=True)
        compete = jnp.dot(piece, kernels[0], preferred_element_type=jnp.float32)
        mutate = jnp.dot(piece, kernels[1], preferred_element_type=jnp.float32)
        compete = compete.astype(jnp.bfloat16)
        mutate = mutate.astype(jnp.bfloat16)
        return (
            compete.astype(jnp.float32).reshape(xcount, ycount, owned),
            mutate.astype(jnp.float32).reshape(xcount, ycount, owned),
        )

    def explicit(padded):
        core = padded[1:-1]
        lapl = padded[2:] + padded[:-2] + jnp.roll(core, 1, 1) + jnp.roll(core, -1, 1) - 4.0 * core
        compete, mutate = products(core)
        return DIFFUSION * lapl + core * (growth - compete) + mutate - core

    padded_pair = with_halo(jnp.stack([section_one, section_two]), (("gx", 1),), 1)
    expl_one = explicit(padded_pair[0])
    expl_two = explicit(padded_pair[1])
    full_one = expl_one - death_rate * section_one
    full_two = expl_two - death_rate * section_two
    result = (
        initial
        + first_dt * death_rate * section_one
        + STEP_SIZE * (5.0 / 12.0 * full_one - 1.0 / 12.0 * full_two)
    ) / (1.0 + first_dt * death_rate)
    new_one, full_one, full_two = (result, full_one, full_two)
    padded_new = with_halo(new_one, (("gx", 0),), 1)
    expl_new = explicit(padded_new)
    new_two = (
        new_one
        + second_dt * (expl_new - expl_one)
        + second_dt * death_rate * section_two
        + STEP_SIZE / 3.0 * (full_one + full_two)
    ) / (1.0 + second_dt * death_rate)
    return (new_one, new_two)


def solution(mesh):
    in_specs = (
        P("gx", None, "trait"),
        P("gx", None, "trait"),
        P("gx", None, "trait"),
        P(None, None, "trait"),
        P("trait"),
        P("trait"),
    )
    out_specs = (P("gx", None, "trait"), P("gx", None, "trait"))
    return jax.shard_map(local, mesh=mesh, in_specs=in_specs, out_specs=out_specs, check_vma=False)
```

profile of v0, /device:TPU:1, one launch (start us, length us, event | category | flops | bytes accessed | tf_op | source)
XLA Modules:
  0.0 153.2 jit_solution(10018028069680694838)
XLA Ops:
  7.2 0.0 all-gather.4.cloned.1.call-start
  7.2 2.2 %convert_element_type.41 = bf16[8,128,256]{2,1,0:T(8,128)(2,1)} convert(f32[8,128,256]{2,1,0:T(8,128)} %param.7) | non-fusion elementwise | flops 262144 | bytes 1572864 | tf_op jit(solution)/shard_map/convert_element_type | solution.py:32
  9.4 0.0 all-gather.4.cloned.1.call-update
  9.5 0.0 copy-start.15
  9.5 0.0 all-gather.6.cloned.1.call-start
  9.5 0.8 convert_element_type.45
  10.4 0.0 all-gather.6.cloned.1.call-update
  10.4 0.0 all-gather.8.cloned.1.call-start
  10.5 16.8 %collective-permute-start = (f32[2,1,128,256]{3,2,1,0:T(8,128)S(1)}, f32[2,1,128,256]{3,2,1,0:T(8,128)S(1)}, u32[]{:S(2)}, u32[]{:S(2)}) collective-permute-start(f32[2,1,128,256]{3,2,1,0:T(8,128)S(1)} %get-tuple-element.6), channel_id=1, source_target_pairs={{4,0},{8,4},{12,8},{16,12},{20,16},{24,20},{28,24},{32,28},{36,32}... | collective-permute-start | bytes 786440 | tf_op jit(solution)/shard_map/ppermute | solution.py:19
  27.3 1.9 %collective-permute-start.1 = (f32[2,1,128,256]{3,2,1,0:T(8,128)S(1)}, f32[2,1,128,256]{3,2,1,0:T(8,128)S(1)}, u32[]{:S(2)}, u32[]{:S(2)}) collective-permute-start(f32[2,1,128,256]{3,2,1,0:T(8,128)S(1)} %get-tuple-element.7), channel_id=1, source_target_pairs={{0,4},{4,8},{8,12},{12,16},{16,20},{20,24},{24,28},{28,32},{32,36}... | collective-permute-start | bytes 786440 | tf_op jit(solution)/shard_map/ppermute | solution.py:17
  29.2 0.6 broadcast_multiply_fusion
  29.9 2.2 %fusion.54 = (f32[8,127,256]{2,1,0:T(8,128)}, f32[8,127,256]{2,1,0:T(8,128)}, f32[8,127,256]{2,1,0:T(8,128)}, f32[8,127,256]{2,1,0:T(8,128)}) fusion(f32[8,128,256]{2,1,0:T(8,128)S(1)} %copy-done.1, f32[8,128,256]{2,1,0:T(8,128)S(1)} %copy-done), kind=kLoop, calls=%fused_computation.76 | loop fusion | bytes 8323072 | tf_op jit(solution)/shard_map/jit(_roll_static)/slice | solution.py:45
  32.0 26.1 %all-gather.4.cloned.1.call-done = bf16[1024,1024]{1,0:T(8,128)(2,1)} async-done(((bf16[1024,256]{1,0:T(8,128)(2,1)}), bf16[1024,1024]{1,0:T(8,128)(2,1)}) %all-gather.4.cloned.1.call-update) | async-done | bytes 2097168 | tf_op jit(solution)/shard_map/all_gather | solution.py:33
  58.2 3.3 %convolution_convert_fusion.4 = bf16[1024,256]{1,0:T(8,128)(2,1)} fusion(bf16[1024,1024]{1,0:T(8,128)(2,1)} %all-gather.4.cloned.1.call-done, bf16[2,1024,256]{2,1,0:T(8,128)(2,1)} %param.9), kind=kOutput, calls=%fused_computation.4 | convolution fusion | flops 537133056 | bytes 3145728 | tf_op jit(solution)/shard_map/dot_general | solution.py:35
  61.5 1.5 convolution_convert_fusion.5
  63.0 29.3 %all-gather.6.cloned.1.call-done = bf16[1024,1024]{1,0:T(8,128)(2,1)} async-done(((bf16[1024,256]{1,0:T(8,128)(2,1)}), bf16[1024,1024]{1,0:T(8,128)(2,1)}) %all-gather.6.cloned.1.call-update) | async-done | bytes 2097168 | tf_op jit(solution)/shard_map/all_gather | solution.py:33
  92.3 2.5 %convolution_convert_fusion.2 = bf16[1024,256]{1,0:T(8,128)(2,1)S(1)} fusion(bf16[1024,1024]{1,0:T(8,128)(2,1)} %all-gather.6.cloned.1.call-done, bf16[2,1024,256]{2,1,0:T(8,128)(2,1)} %param.9), kind=kOutput, calls=%fused_computation.2 | convolution fusion | flops 537133056 | bytes 3145728 | tf_op jit(solution)/shard_map/dot_general | solution.py:35
  94.9 0.1 copy-done.25
  95.0 0.0 copy-start.11
  95.0 0.0 copy-start.17
  95.0 0.7 convolution_convert_fusion.3
  95.7 0.0 collective-permute-done
  95.7 0.0 collective-permute-done.1
  95.8 0.7 copy-done.14
  96.5 0.0 copy-done.8
  96.5 0.4 copy-done.9
  96.9 0.3 copy-done.10
  97.2 0.3 copy-done.11
  97.5 0.1 copy-done.12
  97.7 0.2 copy-done.13
  97.8 3.5 %fusion.47 = (bf16[8,128,256]{2,1,0:T(8,128)(2,1)}, f32[8,128,256]{2,1,0:T(8,128)S(1)}, f32[8,128,256]{2,1,0:T(8,128)}, f32[8,128,256]{2,1,0:T(8,128)}) fusion(f32[256]{0:T(256)S(1)} %get-tuple-element.23, f32[8,128,256]{2,1,0:T(8,128)S(1)} %copy-done, f32[256]{0:T(256)S(1)} %copy-done.15, f32[8,128,256]{2,1,0:T(8,128)S(1)} %copy-done.11, ...), kind=kLoop, calls=%fused_computation.71 | loop fusion | flops 13369344 | bytes 15732736 | tf_op jit(solution)/shard_map/convert_element_type | solution.py:32
  101.4 0.0 all-gather.8.cloned.1.call-update
  101.4 0.7 fusion.52
  102.1 9.9 %collective-permute-start.2 = (f32[1,128,256]{2,1,0:T(8,128)}, f32[1,128,256]{2,1,0:T(8,128)S(1)}, u32[]{:S(2)}, u32[]{:S(2)}) collective-permute-start(f32[1,128,256]{2,1,0:T(8,128)} %get-tuple-element.12), channel_id=1, source_target_pairs={{4,0},{8,4},{12,8},{16,12},{20,16},{24,20},{28,24},{32,28},{36,32}... | collective-permute-start | bytes 393224 | tf_op jit(solution)/shard_map/ppermute | solution.py:19
  112.1 1.9 %collective-permute-start.3 = (f32[1,128,256]{2,1,0:T(8,128)S(1)}, f32[1,128,256]{2,1,0:T(8,128)S(1)}, u32[]{:S(2)}, u32[]{:S(2)}) collective-permute-start(f32[1,128,256]{2,1,0:T(8,128)S(1)} %get-tuple-element.13), channel_id=1, source_target_pairs={{0,4},{4,8},{8,12},{12,16},{16,20},{20,24},{24,28},{28,32},{32,36}... | collective-permute-start | bytes 393224 | tf_op jit(solution)/shard_map/ppermute | solution.py:17
  114.0 1.5 fusion.50
  115.5 24.3 %all-gather.8.cloned.1.call-done = bf16[1024,1024]{1,0:T(8,128)(2,1)} async-done(((bf16[1024,256]{1,0:T(8,128)(2,1)}), bf16[1024,1024]{1,0:T(8,128)(2,1)}) %all-gather.8.cloned.1.call-update) | async-done | bytes 2097168 | tf_op jit(solution)/shard_map/all_gather | solution.py:33
  139.8 2.5 %convolution_convert_fusion = bf16[1024,256]{1,0:T(8,128)(2,1)S(1)} fusion(bf16[1024,1024]{1,0:T(8,128)(2,1)} %all-gather.8.cloned.1.call-done, bf16[2,1024,256]{2,1,0:T(8,128)(2,1)} %param.9), kind=kOutput, calls=%fused_computation | convolution fusion | flops 537133056 | bytes 3145728 | tf_op jit(solution)/shard_map/dot_general | solution.py:35
  142.4 0.1 copy-done.26
  142.5 0.0 copy-start.16
  142.5 0.0 copy-start.18
  142.5 0.7 convolution_convert_fusion.1
  143.2 0.0 collective-permute-done.3
  143.3 0.4 copy-done.3
  143.7 0.3 copy-done.4
  144.0 0.3 copy-done.5
  144.3 0.3 copy-done.6
  144.7 2.0 %fusion.13 = f32[8,128,256]{2,1,0:T(8,128)} fusion(f32[8,128,256]{2,1,0:T(8,128)S(1)} %get-tuple-element.3, f32[8,128,256]{2,1,0:T(8,128)S(1)} %copy-done.3, f32[1,128,256]{2,1,0:T(8,128)S(1)} %collective-permute-done.3, f32[1,128,256]{2,1,0:T(8,128)S(1)} %collective-permute-done.2, f32[8,127,256]{2,1,0:T(8,128)S(1)} %copy-done.6, ...), kind=kLoop, calls=%fused_computation.20 | loop fusion | flops 7340032 | bytes 9703424 | tf_op jit(solution)/shard_map/div | solution.py:62
  (40 shorter events, 0.1 us)
Async XLA Ops:
  7.2 3.3 %copy-start = (f32[8,128,256]{2,1,0:T(8,128)S(1)}, f32[8,128,256]{2,1,0:T(8,128)}, u32[]{:S(2)}) copy-start(f32[8,128,256]{2,1,0:T(8,128)} %param.7) | copy-start | bytes 3145732
  7.2 2.4 %copy-start.1 = (f32[8,128,256]{2,1,0:T(8,128)S(1)}, f32[8,128,256]{2,1,0:T(8,128)}, u32[]{:S(2)}) copy-start(f32[8,128,256]{2,1,0:T(8,128)} %param.8) | copy-start | bytes 3145732
  7.2 51.0 %all-gather.4.cloned.1.call-start = ((), (), s32[]{:S(2)}) async-start(), calls=%async_computation | async-start | bytes 2621440 | tf_op jit(solution)/shard_map/all_gather | solution.py:33
  9.5 19.8 %copy-start.15 = (f32[256]{0:T(256)S(1)}, f32[256]{0:T(256)}, u32[]{:S(2)}) copy-start(f32[256]{0:T(256)} %param.11) | copy-start | bytes 3076
  9.5 82.8 %all-gather.6.cloned.1.call-start = ((), (), s32[]{:S(2)}) async-start(), calls=%async_computation.1 | async-start | bytes 2621440 | tf_op jit(solution)/shard_map/all_gather | solution.py:33
  10.4 129.4 %all-gather.8.cloned.1.call-start = ((), (), s32[]{:S(2)}) async-start(), calls=%async_computation.2 | async-start | bytes 2621440 | tf_op jit(solution)/shard_map/all_gather | solution.py:33
  10.5 85.2 %collective-permute-start = (f32[2,1,128,256]{3,2,1,0:T(8,128)S(1)}, f32[2,1,128,256]{3,2,1,0:T(8,128)S(1)}, u32[]{:S(2)}, u32[]{:S(2)}) collective-permute-start(f32[2,1,128,256]{3,2,1,0:T(8,128)S(1)} %get-tuple-element.6), channel_id=1, source_target_pairs={{4,0},{8,4},{12,8},{16,12},{20,16},{24,20},{28,24},{32,28},{36,32}... | collective-permute-start | bytes 786440 | tf_op jit(solution)/shard_map/ppermute | solution.py:19
  27.3 68.4 %collective-permute-start.1 = (f32[2,1,128,256]{3,2,1,0:T(8,128)S(1)}, f32[2,1,128,256]{3,2,1,0:T(8,128)S(1)}, u32[]{:S(2)}, u32[]{:S(2)}) collective-permute-start(f32[2,1,128,256]{3,2,1,0:T(8,128)S(1)} %get-tuple-element.7), channel_id=1, source_target_pairs={{0,4},{4,8},{8,12},{12,16},{16,20},{20,24},{24,28},{28,32},{32,36}... | collective-permute-start | bytes 786440 | tf_op jit(solution)/shard_map/ppermute | solution.py:17
  58.2 3.3 %copy-start.21 = (bf16[1024,1024]{1,0:T(8,128)(2,1)S(1)}, bf16[1024,1024]{1,0:T(8,128)(2,1)}, u32[]{:S(2)}) copy-start(bf16[1024,1024]{1,0:T(8,128)(2,1)} %all-gather.4.cloned.1.call-done) | copy-start | bytes 6291460
  58.2 3.3 %copy-start.24 = (bf16[2,1024,256]{2,1,0:T(8,128)(2,1)S(1)}, bf16[2,1024,256]{2,1,0:T(8,128)(2,1)}, u32[]{:S(2)}) copy-start(bf16[2,1024,256]{2,1,0:T(8,128)(2,1)} %param.9) | copy-start | bytes 3145732
  92.3 2.5 %copy-start.22 = (bf16[1024,1024]{1,0:T(8,128)(2,1)S(1)}, bf16[1024,1024]{1,0:T(8,128)(2,1)}, u32[]{:S(2)}) copy-start(bf16[1024,1024]{1,0:T(8,128)(2,1)} %all-gather.6.cloned.1.call-done) | copy-start | bytes 6291460
  92.3 2.6 %copy-start.25 = (bf16[2,1024,256]{2,1,0:T(8,128)(2,1)S(1)}, bf16[2,1024,256]{2,1,0:T(8,128)(2,1)}, u32[]{:S(2)}) copy-start(bf16[2,1024,256]{2,1,0:T(8,128)(2,1)} %param.9) | copy-start | bytes 3145732
  95.0 1.5 copy-start.7
  95.0 1.5 %copy-start.8 = (f32[8,127,256]{2,1,0:T(8,128)S(1)}, f32[8,127,256]{2,1,0:T(8,128)}, u32[]{:S(2)}) copy-start(f32[8,127,256]{2,1,0:T(8,128)} %get-tuple-element.17) | copy-start | bytes 3121156
  95.0 1.9 %copy-start.9 = (f32[8,127,256]{2,1,0:T(8,128)S(1)}, f32[8,127,256]{2,1,0:T(8,128)}, u32[]{:S(2)}) copy-start(f32[8,127,256]{2,1,0:T(8,128)} %get-tuple-element.28) | copy-start | bytes 3121156
  95.0 2.3 %copy-start.10 = (f32[8,127,256]{2,1,0:T(8,128)S(1)}, f32[8,127,256]{2,1,0:T(8,128)}, u32[]{:S(2)}) copy-start(f32[8,127,256]{2,1,0:T(8,128)} %get-tuple-element.29) | copy-start | bytes 3121156
  95.0 2.6 %copy-start.11 = (f32[8,128,256]{2,1,0:T(8,128)S(1)}, f32[8,128,256]{2,1,0:T(8,128)}, u32[]{:S(2)}) copy-start(f32[8,128,256]{2,1,0:T(8,128)} %param.6) | copy-start | bytes 3145732
  95.0 2.7 %copy-start.12 = (bf16[1024,256]{1,0:T(8,128)(2,1)S(1)}, bf16[1024,256]{1,0:T(8,128)(2,1)}, u32[]{:S(2)}) copy-start(bf16[1024,256]{1,0:T(8,128)(2,1)} %convolution_convert_fusion.4) | copy-start | bytes 1572868
  95.0 2.8 %copy-start.13 = (bf16[1024,256]{1,0:T(8,128)(2,1)S(1)}, bf16[1024,256]{1,0:T(8,128)(2,1)}, u32[]{:S(2)}) copy-start(bf16[1024,256]{1,0:T(8,128)(2,1)} %convolution_convert_fusion.5) | copy-start | bytes 1572868
  95.0 2.8 %copy-start.17 = (f32[256]{0:T(256)S(1)}, f32[256]{0:T(256)}, u32[]{:S(2)}) copy-start(f32[256]{0:T(256)} %param.10) | copy-start | bytes 3076
  95.7 0.7 copy-start.14
  101.4 41.9 %copy-start.2 = (f32[8,128,256]{2,1,0:T(8,128)}, f32[8,128,256]{2,1,0:T(8,128)S(1)}, u32[]{:S(2)}) copy-start(f32[8,128,256]{2,1,0:T(8,128)S(1)} %get-tuple-element.3) | copy-start | bytes 3145732
  102.1 41.1 %collective-permute-start.2 = (f32[1,128,256]{2,1,0:T(8,128)}, f32[1,128,256]{2,1,0:T(8,128)S(1)}, u32[]{:S(2)}, u32[]{:S(2)}) collective-permute-start(f32[1,128,256]{2,1,0:T(8,128)} %get-tuple-element.12), channel_id=1, source_target_pairs={{4,0},{8,4},{12,8},{16,12},{20,16},{24,20},{28,24},{32,28},{36,32}... | collective-permute-start | bytes 393224 | tf_op jit(solution)/shard_map/ppermute | solution.py:19
  112.1 31.2 %collective-permute-start.3 = (f32[1,128,256]{2,1,0:T(8,128)S(1)}, f32[1,128,256]{2,1,0:T(8,128)S(1)}, u32[]{:S(2)}, u32[]{:S(2)}) collective-permute-start(f32[1,128,256]{2,1,0:T(8,128)S(1)} %get-tuple-element.13), channel_id=1, source_target_pairs={{0,4},{4,8},{8,12},{12,16},{16,20},{20,24},{24,28},{28,32},{32,36}... | collective-permute-start | bytes 393224 | tf_op jit(solution)/shard_map/ppermute | solution.py:17
  139.8 2.5 %copy-start.23 = (bf16[1024,1024]{1,0:T(8,128)(2,1)S(1)}, bf16[1024,1024]{1,0:T(8,128)(2,1)}, u32[]{:S(2)}) copy-start(bf16[1024,1024]{1,0:T(8,128)(2,1)} %all-gather.8.cloned.1.call-done) | copy-start | bytes 6291460
  139.8 2.6 %copy-start.26 = (bf16[2,1024,256]{2,1,0:T(8,128)(2,1)S(1)}, bf16[2,1024,256]{2,1,0:T(8,128)(2,1)}, u32[]{:S(2)}) copy-start(bf16[2,1024,256]{2,1,0:T(8,128)(2,1)} %param.9) | copy-start | bytes 3145732
  142.5 1.2 copy-start.3
  142.5 1.5 %copy-start.4 = (f32[8,128,256]{2,1,0:T(8,128)S(1)}, f32[8,128,256]{2,1,0:T(8,128)}, u32[]{:S(2)}) copy-start(f32[8,128,256]{2,1,0:T(8,128)} %get-tuple-element.5) | copy-start | bytes 3145732
  142.5 1.9 %copy-start.5 = (f32[8,127,256]{2,1,0:T(8,128)S(1)}, f32[8,127,256]{2,1,0:T(8,128)}, u32[]{:S(2)}) copy-start(f32[8,127,256]{2,1,0:T(8,128)} %get-tuple-element.8) | copy-start | bytes 3121156
  142.5 2.2 %copy-start.6 = (f32[8,127,256]{2,1,0:T(8,128)S(1)}, f32[8,127,256]{2,1,0:T(8,128)}, u32[]{:S(2)}) copy-start(f32[8,127,256]{2,1,0:T(8,128)} %get-tuple-element.9) | copy-start | bytes 3121156
  142.5 2.2 %copy-start.16 = (f32[256]{0:T(256)S(1)}, f32[256]{0:T(256)}, u32[]{:S(2)}) copy-start(f32[256]{0:T(256)} %param.11) | copy-start | bytes 3076
  142.5 2.2 %copy-start.18 = (f32[256]{0:T(256)S(1)}, f32[256]{0:T(256)}, u32[]{:S(2)}) copy-start(f32[256]{0:T(256)} %param.10) | copy-start | bytes 3076
  142.5 2.1 %copy-start.19 = (f32[256]{0:T(256)S(1)}, f32[256]{0:T(256)}, u32[]{:S(2)}) copy-start(f32[256]{0:T(256)} %get-tuple-element.22) | copy-start | bytes 3076
  142.5 2.1 %copy-start.20 = (f32[256]{0:T(256)S(1)}, f32[256]{0:T(256)}, u32[]{:S(2)}) copy-start(f32[256]{0:T(256)} %get-tuple-element.24) | copy-start | bytes 3076
Sparse Core Ops, SparseCore 0:
  10.1 48.0 all-gather.3
  60.3 32.0 all-gather.5
  101.5 38.2 all-gather.7
where the time goes:
time: 153 us
  waiting for transfers between devices  79.8 us (52%)
  starting transfers between devices  30.7 us (20%)
  between operations  14 us (9%)
  matrix products  11.3 us (7%)
  other arithmetic  9.25 us (6%)
  local copies, waits for them, and re-layouts  8.15 us (5%)
    all_gather x3, waiting for transfers between devices, products(): piece = lax.all_gather(flat, 'trait', axis=1, tiled=True)  79.7 us
    ppermute x2, starting transfers between devices, with_halo(): lax.ppermute(head, axis, [((i + 1) % count, i) for i in range(count)])  26.7 us
    dot_general x3, matrix products, products(): mutate = jnp.dot(piece, kernels[1], preferred_element_type=jnp.float32)  8.39 us
    convert_element_type x3, other arithmetic, products(): flat = core.astype(jnp.bfloat16).reshape(xcount * ycount, owned)  6.6 us
    ppermute x2, starting transfers between devices, with_halo(): lax.ppermute(tail, axis, [(i, (i + 1) % count) for i in range(count)])  3.84 us
    unnamed x54, local copies, waits for them, and re-layouts  3.7 us
  transfers between devices with their start and end apart: 7, of which 3 were waited for; matrix products, arithmetic and copies ran while one was open for 11% of the time, Pallas kernels for 0%

commit v1 on v0

v1 whole, which is shorter than its diff:
```python
import functools

import jax
import jax.numpy as jnp
from jax import lax
from jax.experimental import pallas as pl
from jax.experimental.pallas import tpu as pltpu
from jax.sharding import PartitionSpec as P

MESH = pl.DeviceIdType.MESH
DIFFUSION = 0.25
STEP_SIZE = 0.5
FIRST_DT = STEP_SIZE / 3.0
SECOND_DT = 2.0 * STEP_SIZE / 3.0

GATHER_ORDER = (0, 7, 1, 2, 3, 4, 5, 6)
FIRST_PLAN = ((), (), (), (1,), (2,), (0, 3), (7, 4), (5,), (6,))
SEND_ORDER = (1, 2, 0, 3, 7, 4, 5, 6)
SECOND_PLAN = ((), (1,), (2,), (), (3,), (), (4, 0), (5, 7), (6,))


def kernel(
    ngx,
    initial, one, two, kernels, growth, death,
    out_one, out_two,
    s_one, s_two, s_init, weights, n_one, rest, sect, news, halo_s, halo_n,
    load_sem, init_sem, weight_sem, out_sem,
    cross_send, cross_recv, pair_send, pair_recv, relay_send, relay_recv, halo_send, halo_recv,
):
    planes, ny, owned = one.shape
    gx = lax.axis_index("gx")
    t = lax.axis_index("trait")
    half = ngx // 2
    pair = t + 1 - 2 * (t % 2)
    cross = (t + 2) % 4
    far = (pair + 2) % 4
    right = (gx + 1) % ngx
    left = (gx + ngx - 1) % ngx
    jump_r = (gx % half + 1) // half
    jump_l = (half - gx % half) // half
    t_r = (t + 2 * jump_r) % 4
    t_l = (t + 2 * jump_l) % 4

    loads = {}
    for p in GATHER_ORDER:
        loads[p] = (
            pltpu.make_async_copy(one.at[p], s_one.at[p], load_sem.at[0, p]),
            pltpu.make_async_copy(two.at[p], s_two.at[p], load_sem.at[1, p]),
        )
        loads[p][0].start()
        loads[p][1].start()
    load_w = pltpu.make_async_copy(kernels, weights, weight_sem)
    load_w.start()
    load_i = pltpu.make_async_copy(initial, s_init, init_sem)
    load_i.start()

    barrier = pltpu.get_barrier_semaphore()
    for device in ((gx, pair), (gx, cross), (right, t_r), (left, t_l)):
        pl.semaphore_signal(barrier, inc=1, device_id=device, device_id_type=MESH)
    pl.semaphore_wait(barrier, 4)

    def remote(src, dst, send, recv, device):
        return pltpu.make_async_remote_copy(
            src_ref=src, dst_ref=dst, send_sem=send, recv_sem=recv, device_id=device, device_id_type=MESH
        )

    started = []

    def start(copy):
        copy.start()
        started.append(copy)

    def spread(buf, s, p):
        mine = buf.at[p, t]
        start(remote(mine, mine, cross_send.at[s, p], cross_recv.at[s, p], (gx, cross)))
        start(remote(mine, mine, pair_send.at[s, p], pair_recv.at[s, p], (gx, pair)))

    def relay(buf, halo, s, p):
        theirs = buf.at[p, cross]
        remote(theirs, theirs, cross_send.at[s, p], cross_recv.at[s, p], (gx, cross)).wait_recv()
        start(remote(theirs, theirs, relay_send.at[s, p], relay_recv.at[s, p], (gx, pair)))
        if p == planes - 1:
            start(remote(buf.at[p, t_r], halo.at[0], halo_send.at[s, 0], halo_recv.at[s, 0], (right, t_r)))
        if p == 0:
            start(remote(buf.at[p, t_l], halo.at[1], halo_send.at[s, 1], halo_recv.at[s, 1], (left, t_l)))

    def gathered(buf, halo, s, p):
        remote(buf.at[p, pair], buf.at[p, pair], pair_send.at[s, p], pair_recv.at[s, p], (gx, pair)).wait_recv()
        remote(buf.at[p, far], buf.at[p, far], relay_send.at[s, p], relay_recv.at[s, p], (gx, pair)).wait_recv()
        if p == 0:
            remote(halo.at[0], halo.at[0], halo_send.at[s, 0], halo_recv.at[s, 0], (left, t_l)).wait_recv()
        if p == planes - 1:
            remote(halo.at[1], halo.at[1], halo_send.at[s, 1], halo_recv.at[s, 1], (right, t_r)).wait_recv()
        rows = jnp.concatenate([buf[p, k] for k in range(4)], axis=1)
        compete = jnp.dot(rows, weights[0], preferred_element_type=jnp.float32)
        mutate = jnp.dot(rows, weights[1], preferred_element_type=jnp.float32)
        return (
            compete.astype(jnp.bfloat16).astype(jnp.float32),
            mutate.astype(jnp.bfloat16).astype(jnp.float32),
        )

    def explicit(field, p, below, above, compete, mutate):
        core = field[p]
        lapl = below + above + pltpu.roll(core, 1, 0) + pltpu.roll(core, ny - 1, 0) - 4.0 * core
        return core, DIFFUSION * lapl + core * (growth[...] - compete) + mutate - core

    def side(field, halo, lo, p):
        if p < 0:
            return halo[0, lo : lo + ny].astype(jnp.float32)
        if p == planes:
            return halo[1, lo : lo + ny].astype(jnp.float32)
        return field[p]

    previous = None
    for p in GATHER_ORDER:
        loads[p][0].wait()
        loads[p][1].wait()
        sect[p, t, :ny] = s_one[p].astype(jnp.bfloat16)
        sect[p, t, ny:] = s_two[p].astype(jnp.bfloat16)
        if previous is not None:
            spread(sect, 0, previous)
        previous = p
    load_w.wait()
    spread(sect, 0, previous)
    load_i.wait()

    rate = death[...]
    scale_one = 1.0 / (1.0 + FIRST_DT * rate)
    scale_two = 1.0 / (1.0 + SECOND_DT * rate)

    def first(p):
        compete, mutate = gathered(sect, halo_s, 0, p)
        v1, e1 = explicit(
            s_one, p, side(s_one, halo_s, 0, p - 1), side(s_one, halo_s, 0, p + 1), compete[:ny], mutate[:ny]
        )
        v2, e2 = explicit(
            s_two, p, side(s_two, halo_s, ny, p - 1), side(s_two, halo_s, ny, p + 1), compete[ny:], mutate[ny:]
        )
        f1 = e1 - rate * v1
        f2 = e2 - rate * v2
        value = (
            s_init[p] + FIRST_DT * rate * v1 + STEP_SIZE * (5.0 / 12.0 * f1 - 1.0 / 12.0 * f2)
        ) * scale_one
        n_one[p] = value
        news[p, t] = value.astype(jnp.bfloat16)
        rest[p] = STEP_SIZE / 3.0 * (e2 - e1 + rate * (v2 - v1))

    writes = []

    def write(src, dst, sem):
        copy = pltpu.make_async_copy(src, dst, sem)
        copy.start()
        writes.append(copy)

    waiting = []

    def flush():
        for p in waiting:
            spread(news, 1, p)
            write(n_one.at[p], out_one.at[p], out_sem.at[0, p])
        waiting.clear()

    for i in range(planes + 1):
        if i < planes:
            relay(sect, halo_s, 0, GATHER_ORDER[i])
        flush()
        for p in FIRST_PLAN[i]:
            first(p)
            flush()
            waiting.append(p)
    flush()

    def second(p):
        compete, mutate = gathered(news, halo_n, 1, p)
        v, e = explicit(n_one, p, side(n_one, halo_n, 0, p - 1), side(n_one, halo_n, 0, p + 1), compete, mutate)
        rest[p] = (v + SECOND_DT * e + rest[p]) * scale_two

    done = []
    for i in range(planes + 1):
        if i < planes:
            relay(news, halo_n, 1, SEND_ORDER[i])
        for p in SECOND_PLAN[i]:
            second(p)
            write(rest.at[p], out_two.at[p], out_sem.at[1, p])
    for copy in started:
        copy.wait_send()
    for copy in writes:
        copy.wait()


def local(ngx, initial, one, two, kernels, growth, death):
    planes, ny, owned = one.shape
    f32, bf16 = jnp.float32, jnp.bfloat16
    hbm = pl.BlockSpec(memory_space=pl.ANY)
    vmem = pl.BlockSpec(memory_space=pltpu.VMEM)
    dma = pltpu.SemaphoreType.DMA
    return pl.pallas_call(
        functools.partial(kernel, ngx),
        out_shape=(jax.ShapeDtypeStruct(one.shape, f32), jax.ShapeDtypeStruct(one.shape, f32)),
        in_specs=[hbm, hbm, hbm, hbm, vmem, vmem],
        out_specs=(hbm, hbm),
        scratch_shapes=[
            pltpu.VMEM(one.shape, f32),
            pltpu.VMEM(one.shape, f32),
            pltpu.VMEM(one.shape, f32),
            pltpu.VMEM(kernels.shape, bf16),
            pltpu.VMEM(one.shape, f32),
            pltpu.VMEM(one.shape, f32),
            pltpu.VMEM((planes, 4, 2 * ny, owned), bf16),
            pltpu.VMEM((planes, 4, ny, owned), bf16),
            pltpu.VMEM((2, 2 * ny, owned), bf16),
            pltpu.VMEM((2, ny, owned), bf16),
            dma((2, planes)),
            dma,
            dma,
            dma((2, planes)),
            dma((2, planes)),
            dma((2, planes)),
            dma((2, planes)),
            dma((2, planes)),
            dma((2, planes)),
            dma((2, planes)),
            dma((2, 2)),
            dma((2, 2)),
        ],
        compiler_params=pltpu.CompilerParams(collective_id=0, has_side_effects=True),
        name="sweep",
    )(initial, one, two, kernels, growth.reshape(1, owned), death.reshape(1, owned))


def solution(mesh):
    field = P("gx", None, "trait")
    return jax.shard_map(
        functools.partial(local, mesh.shape["gx"]),
        mesh=mesh,
        in_specs=(field, field, field, P(None, None, "trait"), P("trait"), P("trait")),
        out_specs=(field, field),
        check_vma=False,
    )
```

time: 153 us -> 59.8 us (0.39)
  waiting for transfers between devices: 79.8 us -> 0 us
  Pallas kernels: 0 us -> 55.7 us
  starting transfers between devices: 30.7 us -> 0 us
  between operations: 14 us -> 0.65 us
  matrix products: 11.3 us -> 0 us
  other arithmetic: 9.25 us -> 0 us
  local copies, waits for them, and re-layouts: 8.15 us -> 3.33 us
    all_gather x3 -> x0, waiting for transfers between devices: 79.7 us -> none  [products(): piece = lax.all_gather(flat, 'trait', axis=1, tiled=True)]
    pallas_call x0 -> x1, Pallas kernels: none -> 55.7 us  [local(): pl.pallas_call(functools.partial(kernel, ngx), out_shape=(jax.ShapeDtypeS...]
    ppermute x4 -> x0, starting transfers between devices: 30.6 us -> none  [the longest x2 26.7 us: with_halo(): lax.ppermute(head, axis, [((i + 1) % count, i) for i in range(count)])]
    dot_general x6 -> x0, matrix products: 11.3 us -> none  [the longest x3 8.39 us: products(): mutate = jnp.dot(piece, kernels[1], preferred_element_type=jnp.float32)]
    convert_element_type x3 -> x0, other arithmetic: 6.6 us -> none  [products(): flat = core.astype(jnp.bfloat16).reshape(xcount * ycount, owned)]
    slice x5 -> x0, local copies, waits for them, and re-layouts: 4.44 us -> none  [the longest x2 2.2 us: explicit(): jnp.roll(core, 1, 1)]
    div x1 -> x0, other arithmetic: 2.01 us -> none  [local(): (new_one + second_dt * (expl_new - expl_one) + second_dt * death_rate * s...]
    unnamed x54 -> x4, local copies, waits for them, and re-layouts: 3.7 us -> 3.33 us
  transfers between devices with their start and end apart: 7 -> 0, of which waited for: 3 -> 0; matrix products, arithmetic and copies ran while one was open for 11% -> 0% of each run, Pallas kernels for 0% -> 0%
where the time goes in v1:
time: 59.8 us; the launch traced here: 59.7 us
  Pallas kernels  55.7 us (93%)
  local copies, waits for them, and re-layouts  3.33 us (6%)
  between operations  0.65 us (1%)
    pallas_call x1, Pallas kernels, local(): pl.pallas_call(functools.partial(kernel, ngx), out_shape=(jax.ShapeDtypeS...  55.7 us
    unnamed x4, local copies, waits for them, and re-layouts  3.33 us

profile of v1, /device:TPU:1, one launch (start us, length us, event | category | flops | bytes accessed | tf_op | source)
XLA Modules:
  0.0 59.7 jit_solution(6698513317707972850)
XLA Ops:
  0.6 55.7 %sweep.1 = (f32[8,128,256]{2,1,0:T(8,128)}, f32[8,128,256]{2,1,0:T(8,128)}) custom-call(f32[8,128,256]{2,1,0:T(8,128)} %initial.1, f32[8,128,256]{2,1,0:T(8,128)} %one.1, f32[8,128,256]{2,1,0:T(8,128)} %two.1, bf16[2,1024,256]{2,1,0:T(8,128)(2,1)} %kernels.1, f32[1,256]{1,0:T(1,128)} %bitcast.2, f32[1,256]{1,0:T(1,128)} %bitcast.3), custom_call_target="tpu_custom_call" | custom-call | tf_op jit(solution)/shard_map/sweep/pallas_call | solution.py:197
  56.3 0.0 copy-start
  56.3 2.4 %copy.10 = f32[8,128,256]{2,1,0:T(8,128)} copy(f32[8,128,256]{2,1,0:T(8,128)} %get-tuple-element.4) | data formatting | bytes 2097152
  58.7 0.0 copy-done
  58.7 1.0 %copy.11 = f32[8,128,256]{2,1,0:T(8,128)} copy(f32[8,128,256]{2,1,0:T(8,128)S(1)} %copy-done) | data formatting | bytes 2097152
Async XLA Ops:
  56.3 2.4 %copy-start = (f32[8,128,256]{2,1,0:T(8,128)S(1)}, f32[8,128,256]{2,1,0:T(8,128)}, u32[]{:S(2)}) copy-start(f32[8,128,256]{2,1,0:T(8,128)} %get-tuple-element.5) | copy-start | bytes 3145732

commit v2 on v1

--- a/solution.py
+++ b/solution.py
@@ -14,17 +14,18 @@
 SECOND_DT = 2.0 * STEP_SIZE / 3.0
 
 GATHER_ORDER = (0, 7, 1, 2, 3, 4, 5, 6)
-FIRST_PLAN = ((), (), (), (1,), (2,), (0, 3), (7, 4), (5,), (6,))
-SEND_ORDER = (1, 2, 0, 3, 7, 4, 5, 6)
-SECOND_PLAN = ((), (1,), (2,), (), (3,), (), (4, 0), (5, 7), (6,))
+FIRST_PLAN = ((), (), (), (1,), (2,), (3, 0, 7), (4,), (5,), (6,))
+SEND_PLAN = ((), (), (), (), (), (0, 7, 1, 2, 3), (4,), (5,), (6,))
+HALO_STEP = 2
+SECOND_PLAN = ((), (), (), (1,), (2,), (3,), (4,), (5, 0, 7), (6,))
 
 
 def kernel(
     ngx,
-    initial, one, two, kernels, growth, death,
-    out_one, out_two,
-    s_one, s_two, s_init, weights, n_one, rest, sect, news, halo_s, halo_n,
-    load_sem, init_sem, weight_sem, out_sem,
+    initial, one, two, kernels, growth_in, death_in,
+    n_one, rest,
+    s_one, s_two, s_init, weights, growth, death, sect, news, halo_s, halo_n,
+    load_sem, init_sem, weight_sem, rate_sem, group_sem, near_sem,
     cross_send, cross_recv, pair_send, pair_recv, relay_send, relay_recv, halo_send, halo_recv,
 ):
     planes, ny, owned = one.shape
@@ -53,11 +54,41 @@
     load_w.start()
     load_i = pltpu.make_async_copy(initial, s_init, init_sem)
     load_i.start()
+    load_g = pltpu.make_async_copy(growth_in, growth, rate_sem.at[0])
+    load_g.start()
+    load_d = pltpu.make_async_copy(death_in, death, rate_sem.at[1])
+    load_d.start()
 
     barrier = pltpu.get_barrier_semaphore()
-    for device in ((gx, pair), (gx, cross), (right, t_r), (left, t_l)):
-        pl.semaphore_signal(barrier, inc=1, device_id=device, device_id_type=MESH)
-    pl.semaphore_wait(barrier, 4)
+    gate = t % 3 == 0
+
+    def greet(sem, *devices):
+        for device in devices:
+            pl.semaphore_signal(sem, inc=1, device_id=device, device_id_type=MESH)
+
+    @pl.when(gate)
+    def _():
+        greet(barrier, (gx, pair), (gx, cross))
+
+    @pl.when(jnp.logical_not(gate))
+    def _():
+        pl.semaphore_wait(barrier, 2)
+        greet(group_sem, (gx, pair), (gx, cross))
+
+    @pl.when(gate)
+    def _():
+        pl.semaphore_wait(group_sem, 2)
+        greet(barrier, (left, t), (right, t))
+
+    def neighbours():
+        @pl.when(gate)
+        def _():
+            pl.semaphore_wait(barrier, 2)
+            greet(near_sem, (gx, pair))
+
+        @pl.when(jnp.logical_not(gate))
+        def _():
+            pl.semaphore_wait(near_sem, 1)
 
     def remote(src, dst, send, recv, device):
         return pltpu.make_async_remote_copy(
@@ -75,10 +106,12 @@
         start(remote(mine, mine, cross_send.at[s, p], cross_recv.at[s, p], (gx, cross)))
         start(remote(mine, mine, pair_send.at[s, p], pair_recv.at[s, p], (gx, pair)))
 
-    def relay(buf, halo, s, p):
+    def relay(buf, s, p):
         theirs = buf.at[p, cross]
         remote(theirs, theirs, cross_send.at[s, p], cross_recv.at[s, p], (gx, cross)).wait_recv()
         start(remote(theirs, theirs, relay_send.at[s, p], relay_recv.at[s, p], (gx, pair)))
+
+    def faces(buf, halo, s, p):
         if p == planes - 1:
             start(remote(buf.at[p, t_r], halo.at[0], halo_send.at[s, 0], halo_recv.at[s, 0], (right, t_r)))
         if p == 0:
@@ -123,6 +156,8 @@
     load_w.wait()
     spread(sect, 0, previous)
     load_i.wait()
+    load_g.wait()
+    load_d.wait()
 
     rate = death[...]
     scale_one = 1.0 / (1.0 + FIRST_DT * rate)
@@ -141,71 +176,56 @@
         value = (
             s_init[p] + FIRST_DT * rate * v1 + STEP_SIZE * (5.0 / 12.0 * f1 - 1.0 / 12.0 * f2)
         ) * scale_one
+        news[p, t] = value.astype(jnp.bfloat16)
         n_one[p] = value
-        news[p, t] = value.astype(jnp.bfloat16)
         rest[p] = STEP_SIZE / 3.0 * (e2 - e1 + rate * (v2 - v1))
-
-    writes = []
-
-    def write(src, dst, sem):
-        copy = pltpu.make_async_copy(src, dst, sem)
-        copy.start()
-        writes.append(copy)
-
-    waiting = []
-
-    def flush():
-        for p in waiting:
-            spread(news, 1, p)
-            write(n_one.at[p], out_one.at[p], out_sem.at[0, p])
-        waiting.clear()
 
     for i in range(planes + 1):
         if i < planes:
-            relay(sect, halo_s, 0, GATHER_ORDER[i])
-        flush()
+            relay(sect, 0, GATHER_ORDER[i])
+        if i == HALO_STEP:
+            neighbours()
+            faces(sect, halo_s, 0, planes - 1)
+            faces(sect, halo_s, 0, 0)
         for p in FIRST_PLAN[i]:
             first(p)
-            flush()
-            waiting.append(p)
-    flush()
+        for p in SEND_PLAN[i]:
+            spread(news, 1, p)
 
     def second(p):
         compete, mutate = gathered(news, halo_n, 1, p)
         v, e = explicit(n_one, p, side(n_one, halo_n, 0, p - 1), side(n_one, halo_n, 0, p + 1), compete, mutate)
         rest[p] = (v + SECOND_DT * e + rest[p]) * scale_two
 
-    done = []
+    order = sum(SEND_PLAN, ())
     for i in range(planes + 1):
         if i < planes:
-            relay(news, halo_n, 1, SEND_ORDER[i])
+            relay(news, 1, order[i])
+            faces(news, halo_n, 1, order[i])
         for p in SECOND_PLAN[i]:
             second(p)
-            write(rest.at[p], out_two.at[p], out_sem.at[1, p])
     for copy in started:
         copy.wait_send()
-    for copy in writes:
-        copy.wait()
 
 
 def local(ngx, initial, one, two, kernels, growth, death):
     planes, ny, owned = one.shape
     f32, bf16 = jnp.float32, jnp.bfloat16
-    hbm = pl.BlockSpec(memory_space=pl.ANY)
+    hbm = pl.BlockSpec(memory_space=pltpu.HBM)
     vmem = pl.BlockSpec(memory_space=pltpu.VMEM)
     dma = pltpu.SemaphoreType.DMA
     return pl.pallas_call(
         functools.partial(kernel, ngx),
         out_shape=(jax.ShapeDtypeStruct(one.shape, f32), jax.ShapeDtypeStruct(one.shape, f32)),
-        in_specs=[hbm, hbm, hbm, hbm, vmem, vmem],
-        out_specs=(hbm, hbm),
+        in_specs=[hbm] * 6,
+        out_specs=(vmem, vmem),
         scratch_shapes=[
             pltpu.VMEM(one.shape, f32),
             pltpu.VMEM(one.shape, f32),
             pltpu.VMEM(one.shape, f32),
             pltpu.VMEM(kernels.shape, bf16),
-            pltpu.VMEM(one.shape, f32),
-            pltpu.VMEM(one.shape, f32),
+            pltpu.VMEM((1, owned), f32),
+            pltpu.VMEM((1, owned), f32),
             pltpu.VMEM((planes, 4, 2 * ny, owned), bf16),
             pltpu.VMEM((planes, 4, ny, owned), bf16),
             pltpu.VMEM((2, 2 * ny, owned), bf16),
@@ -213,7 +233,9 @@
             dma((2, planes)),
             dma,
             dma,
-            dma((2, planes)),
+            dma((2,)),
+            pltpu.SemaphoreType.REGULAR,
+            pltpu.SemaphoreType.REGULAR,
             dma((2, planes)),
             dma((2, planes)),
             dma((2, planes)),
@@ -223,9 +245,14 @@
             dma((2, 2)),
             dma((2, 2)),
         ],
-        compiler_params=pltpu.CompilerParams(collective_id=0, has_side_effects=True),
+        compiler_params=pltpu.CompilerParams(collective_id=0, has_side_effects=True, vmem_limit_bytes=24 * 1024 * 1024),
         name="sweep",
-    )(initial, one, two, kernels, growth.reshape(1, owned), death.reshape(1, owned))
+    )(
+        *[
+            pltpu.with_memory_space_constraint(a, pltpu.HBM)
+            for a in (initial, one, two, kernels, growth.reshape(1, owned), death.reshape(1, owned))
+        ]
+    )
 
 
 def solution(mesh):

time: 59.8 us -> 51.4 us (0.86)
  Pallas kernels: 55.7 us -> 48.7 us
  local copies, waits for them, and re-layouts: 3.33 us -> 1.94 us
    pallas_call x1, Pallas kernels: 55.7 us -> 48.7 us  [local(): pl.pallas_call(functools.partial(kernel, ngx), out_shape=(jax.ShapeDtypeS...]
    unnamed x4 -> x2, local copies, waits for them, and re-layouts: 3.33 us -> 1.94 us
where the time goes in v2:
time: 51.4 us; the launch traced here: 51.2 us
  Pallas kernels  48.7 us (95%)
  local copies, waits for them, and re-layouts  1.94 us (4%)
  between operations  0.64 us (1%)
    pallas_call x1, Pallas kernels, local(): pl.pallas_call(functools.partial(kernel, ngx), out_shape=(jax.ShapeDtypeS...  48.7 us
    unnamed x2, local copies, waits for them, and re-layouts  1.94 us

profile of v2, /device:TPU:1, one launch (start us, length us, event | category | flops | bytes accessed | tf_op | source)
XLA Modules:
  0.0 51.2 jit_solution(11434709350836096380)
XLA Ops:
  0.6 48.7 %sweep.1 = (f32[8,128,256]{2,1,0:T(8,128)S(1)}, f32[8,128,256]{2,1,0:T(8,128)S(1)}) custom-call(f32[8,128,256]{2,1,0:T(8,128)} %initial.1, f32[8,128,256]{2,1,0:T(8,128)} %one.1, f32[8,128,256]{2,1,0:T(8,128)} %two.1, bf16[2,1024,256]{2,1,0:T(8,128)(2,1)} %kernels.1, f32[1,256]{1,0:T(1,128)} %bitcast.2, f32[1,256]{1,0:T(1,128)} %bitcast.3), custom_call_target="tpu_custom_call" | custom-call | tf_op jit(solution)/shard_map/sweep/pallas_call | solution.py:217
  49.3 1.0 %copy.10 = f32[8,128,256]{2,1,0:T(8,128)} copy(f32[8,128,256]{2,1,0:T(8,128)S(1)} %get-tuple-element.4) | data formatting | bytes 2097152
  50.3 1.0 %copy.11 = f32[8,128,256]{2,1,0:T(8,128)} copy(f32[8,128,256]{2,1,0:T(8,128)S(1)} %get-tuple-element.5) | data formatting | bytes 2097152

commit v3 on v2

--- a/solution.py
+++ b/solution.py
@@ -25,7 +25,7 @@
     initial, one, two, kernels, growth_in, death_in,
     n_one, rest,
     s_one, s_two, s_init, weights, growth, death, sect, news, halo_s, halo_n,
-    load_sem, init_sem, weight_sem, rate_sem, group_sem, near_sem,
+    load_sem, init_sem, weight_sem, rate_sem, cross_sem, pair_sem, near_sem,
     cross_send, cross_recv, pair_send, pair_recv, relay_send, relay_recv, halo_send, halo_recv,
 ):
     planes, ny, owned = one.shape
@@ -60,33 +60,56 @@
     load_d.start()
 
     barrier = pltpu.get_barrier_semaphore()
-    gate = t % 3 == 0
 
     def greet(sem, *devices):
         for device in devices:
             pl.semaphore_signal(sem, inc=1, device_id=device, device_id_type=MESH)
 
-    @pl.when(gate)
-    def _():
-        greet(barrier, (gx, pair), (gx, cross))
-
-    @pl.when(jnp.logical_not(gate))
+    @pl.when(t == 3)
+    def _():
+        greet(barrier, (gx, cross), (gx, pair))
+
+    @pl.when(t == 1)
+    def _():
+        greet(barrier, (gx, pair))
+
+    @pl.when(t == 0)
+    def _():
+        greet(barrier, (gx, cross))
+        pl.semaphore_wait(barrier, 1)
+        greet(pair_sem, (gx, pair))
+
+    @pl.when(t == 1)
+    def _():
+        pl.semaphore_wait(barrier, 1)
+        greet(cross_sem, (gx, cross))
+
+    @pl.when(t == 2)
     def _():
         pl.semaphore_wait(barrier, 2)
-        greet(group_sem, (gx, pair), (gx, cross))
-
-    @pl.when(gate)
-    def _():
-        pl.semaphore_wait(group_sem, 2)
-        greet(barrier, (left, t), (right, t))
+        greet(cross_sem, (gx, cross))
+        greet(pair_sem, (gx, pair))
+
+    @pl.when(t % 3 == 0)
+    def _():
+        pl.semaphore_wait(cross_sem, 1)
+
+    def paired():
+        @pl.when(t % 2 == 1)
+        def _():
+            pl.semaphore_wait(pair_sem, 1)
+
+        @pl.when(t == 3)
+        def _():
+            greet(barrier, (left, t), (right, t))
 
     def neighbours():
-        @pl.when(gate)
+        @pl.when(t == 3)
         def _():
             pl.semaphore_wait(barrier, 2)
-            greet(near_sem, (gx, pair))
-
-        @pl.when(jnp.logical_not(gate))
+            greet(near_sem, (gx, pair), (gx, cross), (gx, far))
+
+        @pl.when(t != 3)
         def _():
             pl.semaphore_wait(near_sem, 1)
 
@@ -101,9 +124,12 @@
         copy.start()
         started.append(copy)
 
-    def spread(buf, s, p):
+    def to_cross(buf, s, p):
         mine = buf.at[p, t]
         start(remote(mine, mine, cross_send.at[s, p], cross_recv.at[s, p], (gx, cross)))
+
+    def to_pair(buf, s, p):
+        mine = buf.at[p, t]
         start(remote(mine, mine, pair_send.at[s, p], pair_recv.at[s, p], (gx, pair)))
 
     def relay(buf, s, p):
@@ -151,10 +177,13 @@
         sect[p, t, :ny] = s_one[p].astype(jnp.bfloat16)
         sect[p, t, ny:] = s_two[p].astype(jnp.bfloat16)
         if previous is not None:
-            spread(sect, 0, previous)
+            to_cross(sect, 0, previous)
         previous = p
     load_w.wait()
-    spread(sect, 0, previous)
+    to_cross(sect, 0, previous)
+    paired()
+    for p in GATHER_ORDER:
+        to_pair(sect, 0, p)
     load_i.wait()
     load_g.wait()
     load_d.wait()
@@ -190,7 +219,8 @@
         for p in FIRST_PLAN[i]:
             first(p)
         for p in SEND_PLAN[i]:
-            spread(news, 1, p)
+            to_cross(news, 1, p)
+            to_pair(news, 1, p)
 
     def second(p):
         compete, mutate = gathered(news, halo_n, 1, p)
@@ -208,13 +238,24 @@
         copy.wait_send()
 
 
+def store(value_one, value_two, out_one, out_two, sem):
+    copies = (
+        pltpu.make_async_copy(value_one, out_one, sem.at[0]),
+        pltpu.make_async_copy(value_two, out_two, sem.at[1]),
+    )
+    for copy in copies:
+        copy.start()
+    for copy in copies:
+        copy.wait()
+
+
 def local(ngx, initial, one, two, kernels, growth, death):
     planes, ny, owned = one.shape
     f32, bf16 = jnp.float32, jnp.bfloat16
     hbm = pl.BlockSpec(memory_space=pltpu.HBM)
     vmem = pl.BlockSpec(memory_space=pltpu.VMEM)
     dma = pltpu.SemaphoreType.DMA
-    return pl.pallas_call(
+    results = pl.pallas_call(
         functools.partial(kernel, ngx),
         out_shape=(jax.ShapeDtypeStruct(one.shape, f32), jax.ShapeDtypeStruct(one.shape, f32)),
         in_specs=[hbm] * 6,
@@ -236,6 +277,7 @@
             dma((2,)),
             pltpu.SemaphoreType.REGULAR,
             pltpu.SemaphoreType.REGULAR,
+            pltpu.SemaphoreType.REGULAR,
             dma((2, planes)),
             dma((2, planes)),
             dma((2, planes)),
@@ -253,6 +295,15 @@
             for a in (initial, one, two, kernels, growth.reshape(1, owned), death.reshape(1, owned))
         ]
     )
+    return pl.pallas_call(
+        store,
+        out_shape=(jax.ShapeDtypeStruct(one.shape, f32), jax.ShapeDtypeStruct(one.shape, f32)),
+        in_specs=[vmem, vmem],
+        out_specs=(pl.BlockSpec(memory_space=pl.ANY), pl.BlockSpec(memory_space=pl.ANY)),
+        scratch_shapes=[dma((2,))],
+        compiler_params=pltpu.CompilerParams(vmem_limit_bytes=8 * 1024 * 1024),
+        name="store",
+    )(*[a for a in results])
 
 
 def solution(mesh):

time: 51.4 us -> 50 us (0.973)
  local copies, waits for them, and re-layouts: 1.94 us -> 0 us
    unnamed x2 -> x0, local copies, waits for them, and re-layouts: 1.94 us -> none
    pallas_call x0 -> x1, Pallas kernels: none -> 1.33 us  [local(): pl.pallas_call(store, out_shape=(jax.ShapeDtypeStruct(one.shape, f32), ja...]
    pallas_call x1, Pallas kernels: 48.7 us -> 47.9 us  [local(): pl.pallas_call(functools.partial(kernel, ngx), out_shape=(jax.ShapeDtypeS...]
where the time goes in v3:
time: 50 us; the launch traced here: 49.9 us
  Pallas kernels  49.2 us (98%)
  between operations  0.64 us (1%)
    pallas_call x1, Pallas kernels, local(): pl.pallas_call(functools.partial(kernel, ngx), out_shape=(jax.ShapeDtypeS...  47.9 us
    pallas_call x1, Pallas kernels, local(): pl.pallas_call(store, out_shape=(jax.ShapeDtypeStruct(one.shape, f32), ja...  1.33 us

profile of v3, /device:TPU:1, one launch (start us, length us, event | category | flops | bytes accessed | tf_op | source)
XLA Modules:
  0.0 49.9 jit_solution(6740369550427633977)
XLA Ops:
  0.6 47.9 %sweep.1 = (f32[8,128,256]{2,1,0:T(8,128)S(1)}, f32[8,128,256]{2,1,0:T(8,128)S(1)}) custom-call(f32[8,128,256]{2,1,0:T(8,128)} %initial.1, f32[8,128,256]{2,1,0:T(8,128)} %one.1, f32[8,128,256]{2,1,0:T(8,128)} %two.1, bf16[2,1024,256]{2,1,0:T(8,128)(2,1)} %kernels.1, f32[1,256]{1,0:T(1,128)} %bitcast.2, f32[1,256]{1,0:T(1,128)} %bitcast.3), custom_call_target="tpu_custom_call" | custom-call | tf_op jit(solution)/shard_map/sweep/pallas_call | solution.py:258
  48.5 1.3 %store.1 = (f32[8,128,256]{2,1,0:T(8,128)}, f32[8,128,256]{2,1,0:T(8,128)}) custom-call(f32[8,128,256]{2,1,0:T(8,128)S(1)} %get-tuple-element.4.value_one, f32[8,128,256]{2,1,0:T(8,128)S(1)} %get-tuple-element.5.value_two), custom_call_target="tpu_custom_call" | custom-call | tf_op jit(solution)/shard_map/store/pallas_call | solution.py:298

commit v4 on v3

--- a/solution.py
+++ b/solution.py
@@ -14,10 +14,10 @@
 SECOND_DT = 2.0 * STEP_SIZE / 3.0
 
 GATHER_ORDER = (0, 7, 1, 2, 3, 4, 5, 6)
-FIRST_PLAN = ((), (), (), (1,), (2,), (3, 0, 7), (4,), (5,), (6,))
-SEND_PLAN = ((), (), (), (), (), (0, 7, 1, 2, 3), (4,), (5,), (6,))
+FIRST_PLAN = ((), (), (), (1,), (0, 2), (7, 3), (4,), (5,), (6,))
+SEND_PLAN = ((), (), (), (), (0,), (7, 1, 2, 3), (4,), (5,), (6,))
 HALO_STEP = 2
-SECOND_PLAN = ((), (), (), (1,), (2,), (3,), (4,), (5, 0, 7), (6,))
+SECOND_PLAN = ((), (), (), (1,), (2,), (3, 0), (4, 7), (5,), (6,))
 
 
 def kernel(
@@ -239,10 +239,10 @@
 
 
 def store(value_one, value_two, out_one, out_two, sem):
-    copies = (
-        pltpu.make_async_copy(value_one, out_one, sem.at[0]),
-        pltpu.make_async_copy(value_two, out_two, sem.at[1]),
-    )
+    copies = []
+    for p in range(value_one.shape[0]):
+        copies.append(pltpu.make_async_copy(value_one.at[p], out_one.at[p], sem.at[0, p]))
+        copies.append(pltpu.make_async_copy(value_two.at[p], out_two.at[p], sem.at[1, p]))
     for copy in copies:
         copy.start()
     for copy in copies:
@@ -300,7 +300,7 @@
         out_shape=(jax.ShapeDtypeStruct(one.shape, f32), jax.ShapeDtypeStruct(one.shape, f32)),
         in_specs=[vmem, vmem],
         out_specs=(pl.BlockSpec(memory_space=pl.ANY), pl.BlockSpec(memory_space=pl.ANY)),
-        scratch_shapes=[dma((2,))],
+        scratch_shapes=[dma((2, planes))],
         compiler_params=pltpu.CompilerParams(vmem_limit_bytes=8 * 1024 * 1024),
         name="store",
     )(*[a for a in results])

time: 50 us -> 53.9 us (1.078)
  Pallas kernels: 49.2 us -> 53.1 us
    pallas_call x1, Pallas kernels: 47.9 us -> 51.7 us  [local(): pl.pallas_call(functools.partial(kernel, ngx), out_shape=(jax.ShapeDtypeS...]
where the time goes in v4:
time: 53.9 us; the launch traced here: 53.7 us
  Pallas kernels  53.1 us (99%)
  between operations  0.64 us (1%)
    pallas_call x1, Pallas kernels, local(): pl.pallas_call(functools.partial(kernel, ngx), out_shape=(jax.ShapeDtypeS...  51.7 us
    pallas_call x1, Pallas kernels, local(): pl.pallas_call(store, out_shape=(jax.ShapeDtypeStruct(one.shape, f32), ja...  1.44 us

profile of v4, /device:TPU:1, one launch (start us, length us, event | category | flops | bytes accessed | tf_op | source)
XLA Modules:
  0.0 53.7 jit_solution(14453850281469781377)
XLA Ops:
  0.6 51.7 %sweep.1 = (f32[8,128,256]{2,1,0:T(8,128)S(1)}, f32[8,128,256]{2,1,0:T(8,128)S(1)}) custom-call(f32[8,128,256]{2,1,0:T(8,128)} %initial.1, f32[8,128,256]{2,1,0:T(8,128)} %one.1, f32[8,128,256]{2,1,0:T(8,128)} %two.1, bf16[2,1024,256]{2,1,0:T(8,128)(2,1)} %kernels.1, f32[1,256]{1,0:T(1,128)} %bitcast.2, f32[1,256]{1,0:T(1,128)} %bitcast.3), custom_call_target="tpu_custom_call" | custom-call | tf_op jit(solution)/shard_map/sweep/pallas_call | solution.py:258
  52.3 1.4 %store.1 = (f32[8,128,256]{2,1,0:T(8,128)}, f32[8,128,256]{2,1,0:T(8,128)}) custom-call(f32[8,128,256]{2,1,0:T(8,128)S(1)} %get-tuple-element.4.value_one, f32[8,128,256]{2,1,0:T(8,128)S(1)} %get-tuple-element.5.value_two), custom_call_target="tpu_custom_call" | custom-call | tf_op jit(solution)/shard_map/store/pallas_call | solution.py:298

commit v5 on v3

--- a/solution.py
+++ b/solution.py
@@ -14,10 +14,10 @@
 SECOND_DT = 2.0 * STEP_SIZE / 3.0
 
 GATHER_ORDER = (0, 7, 1, 2, 3, 4, 5, 6)
-FIRST_PLAN = ((), (), (), (1,), (2,), (3, 0, 7), (4,), (5,), (6,))
-SEND_PLAN = ((), (), (), (), (), (0, 7, 1, 2, 3), (4,), (5,), (6,))
+FIRST_PLAN = ((), (), (), (1,), (0, 2), (7, 3), (4,), (5,), (6,))
+SEND_PLAN = ((), (), (), (), (0,), (7, 1, 2, 3), (4,), (5,), (6,))
 HALO_STEP = 2
-SECOND_PLAN = ((), (), (), (1,), (2,), (3,), (4,), (5, 0, 7), (6,))
+SECOND_PLAN = ((), (), (), (1,), (2,), (3, 0), (4, 7), (5,), (6,))
 
 
 def kernel(
@@ -42,6 +42,24 @@
     t_r = (t + 2 * jump_r) % 4
     t_l = (t + 2 * jump_l) % 4
 
+    barrier = pltpu.get_barrier_semaphore()
+
+    def greet(sem, *devices):
+        for device in devices:
+            pl.semaphore_signal(sem, inc=1, device_id=device, device_id_type=MESH)
+
+    @pl.when(t == 3)
+    def _():
+        greet(barrier, (gx, cross), (gx, pair))
+
+    @pl.when(t == 1)
+    def _():
+        greet(barrier, (gx, pair))
+
+    @pl.when(t == 0)
+    def _():
+        greet(barrier, (gx, cross))
+
     loads = {}
     for p in GATHER_ORDER:
         loads[p] = (
@@ -59,23 +77,8 @@
     load_d = pltpu.make_async_copy(death_in, death, rate_sem.at[1])
     load_d.start()
 
-    barrier = pltpu.get_barrier_semaphore()
-
-    def greet(sem, *devices):
-        for device in devices:
-            pl.semaphore_signal(sem, inc=1, device_id=device, device_id_type=MESH)
-
-    @pl.when(t == 3)
-    def _():
-        greet(barrier, (gx, cross), (gx, pair))
-
-    @pl.when(t == 1)
-    def _():
-        greet(barrier, (gx, pair))
-
     @pl.when(t == 0)
     def _():
-        greet(barrier, (gx, cross))
         pl.semaphore_wait(barrier, 1)
         greet(pair_sem, (gx, pair))
 

time: 50 us -> 53.7 us (1.074)
  Pallas kernels: 49.2 us -> 53 us
    pallas_call x1, Pallas kernels: 47.9 us -> 51.6 us  [local(): pl.pallas_call(functools.partial(kernel, ngx), out_shape=(jax.ShapeDtypeS...]
where the time goes in v5:
time: 53.7 us; the launch traced here: 53.6 us
  Pallas kernels  53 us (99%)
  between operations  0.64 us (1%)
    pallas_call x1, Pallas kernels, local(): pl.pallas_call(functools.partial(kernel, ngx), out_shape=(jax.ShapeDtypeS...  51.6 us
    pallas_call x1, Pallas kernels, local(): pl.pallas_call(store, out_shape=(jax.ShapeDtypeStruct(one.shape, f32), ja...  1.33 us

profile of v5, /device:TPU:1, one launch (start us, length us, event | category | flops | bytes accessed | tf_op | source)
XLA Modules:
  0.0 53.6 jit_solution(10195680627884626151)
XLA Ops:
  0.6 51.6 %sweep.1 = (f32[8,128,256]{2,1,0:T(8,128)S(1)}, f32[8,128,256]{2,1,0:T(8,128)S(1)}) custom-call(f32[8,128,256]{2,1,0:T(8,128)} %initial.1, f32[8,128,256]{2,1,0:T(8,128)} %one.1, f32[8,128,256]{2,1,0:T(8,128)} %two.1, bf16[2,1024,256]{2,1,0:T(8,128)(2,1)} %kernels.1, f32[1,256]{1,0:T(1,128)} %bitcast.2, f32[1,256]{1,0:T(1,128)} %bitcast.3), custom_call_target="tpu_custom_call" | custom-call | tf_op jit(solution)/shard_map/sweep/pallas_call | solution.py:261
  52.3 1.3 %store.1 = (f32[8,128,256]{2,1,0:T(8,128)}, f32[8,128,256]{2,1,0:T(8,128)}) custom-call(f32[8,128,256]{2,1,0:T(8,128)S(1)} %get-tuple-element.4.value_one, f32[8,128,256]{2,1,0:T(8,128)S(1)} %get-tuple-element.5.value_two), custom_call_target="tpu_custom_call" | custom-call | tf_op jit(solution)/shard_map/store/pallas_call | solution.py:301
